TPU v7x, 256 devices: a whole 4x4x8 slice. The times are simulated.
256 devices in a mesh: gx: 16 (over z, core), gy: 16 (over x, y).
Axes of the slice: x: 4, y: 4, z: 8, core: 2. Of those that a mesh axis runs over, the one named last changes fastest.
Arguments:
- right_sides: float32 [16384, 8, 128], P(('gx', 'gy')), may hold values from -30 to 30
- diag_blocks: bfloat16 [16384, 128, 128], P(('gx', 'gy')), may hold values from -1 to 2
- face_blocks: bfloat16 [16384, 4, 128, 128], P(('gx', 'gy')), may hold values from -0.125 to 0.125
- neighbours: int32 [16384, 4], P(('gx', 'gy')), may hold values from -1 to 207, as said below
- send_slots: int32 [256, 9, 16], P(('gx', 'gy')), may hold values from -1 to 63, as said below
- counts: int32 [256], P(('gx', 'gy')), may hold values from 32 to 64, as said below
Outputs:
- solution: float32 [16384, 8, 128], P(('gx', 'gy'))
- residual: float32 [16384, 8, 128], P(('gx', 'gy'))
Inputs may be any that keep to these rules, and one draw needn't show every extreme that they name: The first counts[g] slots of group g hold its elements; some group has exactly 64. send_slots[g, d, k] is a live slot of group g whose vector group g sends, as its k-th ghost of direction d = 3 (dx + 1) + (dy + 1), to the group at grid offset (dx, dy); -1 marks no block. A list's live entries come first and are distinct; direction 4 and directions leaving the grid hold only -1; some list holds 16 live entries. neighbours[e, f] is -1 (no coupling), a live slot of the same group, or 64 + d * 16 + k naming a live entry k of direction d of the sending group at offset -(dx, dy); slots at or beyond counts hold only -1.
All inputs are finite; a program needn't handle non-finite values.
Results may differ from a plain program's by a relative error of at most 0.0075.
The roundings to bfloat16 on the way count: a program that leaves them out, or rounds other values in their place, can miss the bound.
Values may be sent and summed in bfloat16 or wider, within the bound.
No kernel may reach another device: no remote copies, remote signals or barrier semaphores. Data moves between devices by JAX's collectives and lax.ppermute only.
A program may use at most 64 MiB of HBM per device.

v0:
```python
import jax
import jax.numpy as jnp
from jax import lax
from jax.sharding import PartitionSpec as P

POWERS = 4
HIGH = lax.Precision.HIGHEST


def passed_along(block, axis, distance):
    devices = range(lax.axis_size(axis))
    route = [(i - distance, i) for i in devices if i - distance in devices]
    return lax.ppermute(block, axis, route)


def forward_solve(factor, values):
    extent = factor.shape[-1]
    result = []
    for row_at in range(extent):
        running = values[:, row_at]
        for col_at in range(row_at):
            running = running - factor[:, row_at, col_at] * result[col_at]
        result.append(running / factor[:, row_at, row_at])
    return jnp.stack(result, axis=1)


def backward_solve(factor, values):
    extent = factor.shape[-1]
    result = [None] * extent
    for row_at in reversed(range(extent)):
        running = values[:, row_at]
        for col_at in range(row_at + 1, extent):
            running = running - factor[:, col_at, row_at] * result[col_at]
        result[row_at] = running / factor[:, row_at, row_at]
    return jnp.stack(result, axis=1)


def coefficients(gram):
    factor = jnp.linalg.cholesky(gram[:, 1:, 1:])
    return backward_solve(factor, forward_solve(factor, gram[:, 1:, 0]))


def fetch_ghosts(packets):
    empty = jnp.zeros_like(packets[4])
    columns = lax.axis_size("gy")
    column = lax.axis_index("gy")
    arrived = []
    for target in range(9):
        if target == 4:
            arrived.append(empty)
        else:
            step_row = target // 3 - 1
            step_col = target % 3 - 1
            shifted = passed_along(packets[target], ("gx", "gy"), step_row * columns + step_col)
            inside = (column - step_col >= 0) & (column - step_col < columns)
            arrived.append(jnp.where(inside, shifted, jnp.zeros((), jnp.bfloat16)))
    return jnp.stack(arrived)


def per_device(right_sides, diag_blocks, face_blocks, neighbours, send_slots, counts):
    capacity = right_sides.shape[0]
    slot_ids = lax.iota(jnp.int32, capacity)
    live_mask = (slot_ids < counts[0]).astype(jnp.float32)[:, None, None]
    outgoing = send_slots[0]
    sending = outgoing >= 0
    out_index = jnp.where(sending, outgoing, 0)
    present = neighbours >= 0
    source = jnp.where(present, neighbours, 0)
    zero_half = jnp.zeros((), jnp.bfloat16)
    vectors = [right_sides * live_mask]
    for step_index in range(POWERS):
        rounded = vectors[-1].astype(jnp.bfloat16)
        packets = jnp.where(sending[:, :, None, None], rounded[out_index], zero_half)
        ghosts = fetch_ghosts(packets)
        lookup = jnp.concatenate([rounded, ghosts.reshape((-1,) + rounded.shape[1:])], axis=0)
        gathered = jnp.where(present[:, :, None, None], lookup[source], zero_half)
        own_part = jnp.einsum(
            "eij,erj->eri", diag_blocks, rounded, preferred_element_type=jnp.float32
        )
        face_part = jnp.einsum(
            "efij,efrj->eri", face_blocks, gathered, preferred_element_type=jnp.float32
        )
        vectors.append((own_part + face_part) * live_mask)
    basis = jnp.stack(vectors)
    local_gram = jnp.einsum("icrn,jcrn->rij", basis, basis, precision=HIGH)
    gram = lax.psum(local_gram, ("gx", "gy"))
    weights = coefficients(gram)
    solution = jnp.einsum("rk,kcrn->crn", weights, basis[:POWERS], precision=HIGH)
    residual = basis[0] - jnp.einsum("rk,kcrn->crn", weights, basis[1:], precision=HIGH)
    return (solution, residual)


def solution(mesh):
    in_specs = (
        P(("gx", "gy"), None, None),
        P(("gx", "gy"), None, None),
        P(("gx", "gy"), None, None, None),
        P(("gx", "gy"), None),
        P(("gx", "gy"), None, None),
        P(("gx", "gy")),
    )
    out_specs = (P(("gx", "gy"), None, None), P(("gx", "gy"), None, None))
    return jax.shard_map(
        per_device, mesh=mesh, in_specs=in_specs, out_specs=out_specs, check_vma=False
    )
```

profile of v0, /device:TPU:1, one launch (start us, length us, event | category | flops | bytes accessed | tf_op | source)
XLA Modules:
  0.0 309.1 jit_solution(4113129172325548190)
XLA Ops:
  7.9 5.1 %collective-permute-start.1 = (bf16[16,8,128]{2,1,0:T(8,128)(2,1)}, bf16[16,8,128]{2,1,0:T(8,128)(2,1)}, u32[]{:S(2)}, u32[]{:S(2)}) collective-permute-start(bf16[16,8,128]{2,1,0:T(8,128)(2,1)} %get-tuple-element.53), channel_id=1, source_target_pairs={{16,0},{17,1},{18,2},{19,3},{20,4},{21,5},{22,6},{23,7},{24,8},{25... | collective-permute-start | bytes 98312 | tf_op jit(solution)/shard_map/ppermute | solution.py:13
  13.1 1.9 collective-permute-start.2
  15.0 6.2 %collective-permute-start.3 = (bf16[16,8,128]{2,1,0:T(8,128)(2,1)}, bf16[16,8,128]{2,1,0:T(8,128)(2,1)}, u32[]{:S(2)}, u32[]{:S(2)}) collective-permute-start(bf16[16,8,128]{2,1,0:T(8,128)(2,1)} %get-tuple-element.51), channel_id=1, source_target_pairs={{1,0},{2,1},{3,2},{4,3},{5,4},{6,5},{7,6},{8,7},{9,8},{10,9},{11,1... | collective-permute-start | bytes 98312 | tf_op jit(solution)/shard_map/ppermute | solution.py:13
  21.2 1.9 collective-permute-start.4
  26.2 8.3 %collective-permute-start.5 = (bf16[16,8,128]{2,1,0:T(8,128)(2,1)}, bf16[16,8,128]{2,1,0:T(8,128)(2,1)S(1)}, u32[]{:S(2)}, u32[]{:S(2)}) collective-permute-start(bf16[16,8,128]{2,1,0:T(8,128)(2,1)} %get-tuple-element.49), channel_id=1, source_target_pairs={{0,15},{1,16},{2,17},{3,18},{4,19},{5,20},{6,21},{7,22},{8,23},{9,... | collective-permute-start | bytes 98312 | tf_op jit(solution)/shard_map/ppermute | solution.py:13
  35.3 6.7 %collective-permute-start.6 = (bf16[16,8,128]{2,1,0:T(8,128)(2,1)}, bf16[16,8,128]{2,1,0:T(8,128)(2,1)S(1)}, u32[]{:S(2)}, u32[]{:S(2)}) collective-permute-start(bf16[16,8,128]{2,1,0:T(8,128)(2,1)} %get-tuple-element.48), channel_id=1, source_target_pairs={{0,16},{1,17},{2,18},{3,19},{4,20},{5,21},{6,22},{7,23},{8,24},{9,... | collective-permute-start | bytes 98312 | tf_op jit(solution)/shard_map/ppermute | solution.py:13
  46.3 2.6 gather_fusion.1
  48.9 5.9 %convolution_bitcast_fusion.3 = f32[64,8,128]{2,1,0:T(8,128)S(1)} fusion(bf16[64,4,128,128]{3,2,1,0:T(8,128)(2,1)} %param.8, bf16[64,4,8,128]{3,2,1,0:T(8,128)(2,1)} %bitcast.295, pred[64,4]{1,0:T(8,128)(4,1)S(1)} %copy.36), kind=kOutput, calls=%fused_computation.20 | convolution fusion | flops 67371008 | bytes 9175296 | tf_op jit(solution)/shard_map/efij,efrj->eri/dot_general | solution.py:80
  60.7 1.9 collective-permute-start.9
  64.5 8.1 %collective-permute-start.11 = (bf16[16,8,128]{2,1,0:T(8,128)(2,1)S(1)}, bf16[16,8,128]{2,1,0:T(8,128)(2,1)S(1)}, u32[]{:S(2)}, u32[]{:S(2)}) collective-permute-start(bf16[16,8,128]{2,1,0:T(8,128)(2,1)S(1)} %get-tuple-element.43), channel_id=1, source_target_pairs={{1,0},{2,1},{3,2},{4,3},{5,4},{6,5},{7,6},{8,7},{9,8},{10,9},{11,1... | collective-permute-start | bytes 98312 | tf_op jit(solution)/shard_map/ppermute | solution.py:13
  72.6 1.9 collective-permute-start.12
  74.5 9.5 %collective-permute-start.13 = (bf16[16,8,128]{2,1,0:T(8,128)(2,1)S(1)}, bf16[16,8,128]{2,1,0:T(8,128)(2,1)S(1)}, u32[]{:S(2)}, u32[]{:S(2)}) collective-permute-start(bf16[16,8,128]{2,1,0:T(8,128)(2,1)S(1)} %get-tuple-element.41), channel_id=1, source_target_pairs={{0,15},{1,16},{2,17},{3,18},{4,19},{5,20},{6,21},{7,22},{8,23},{9,... | collective-permute-start | bytes 98312 | tf_op jit(solution)/shard_map/ppermute | solution.py:13
  84.1 7.8 %collective-permute-start.14 = (bf16[16,8,128]{2,1,0:T(8,128)(2,1)S(1)}, bf16[16,8,128]{2,1,0:T(8,128)(2,1)S(1)}, u32[]{:S(2)}, u32[]{:S(2)}) collective-permute-start(bf16[16,8,128]{2,1,0:T(8,128)(2,1)S(1)} %get-tuple-element.40), channel_id=1, source_target_pairs={{0,16},{1,17},{2,18},{3,19},{4,20},{5,21},{6,22},{7,23},{8,24},{9,... | collective-permute-start | bytes 98312 | tf_op jit(solution)/shard_map/ppermute | solution.py:13
  95.0 2.6 gather_fusion.3
  97.6 5.9 %convolution_bitcast_fusion.2 = f32[64,8,128]{2,1,0:T(8,128)S(1)} fusion(bf16[64,4,128,128]{3,2,1,0:T(8,128)(2,1)} %param.8, bf16[64,4,8,128]{3,2,1,0:T(8,128)(2,1)} %bitcast.296, pred[64,4]{1,0:T(8,128)(4,1)S(1)} %copy.36), kind=kOutput, calls=%fused_computation.17 | convolution fusion | flops 67371008 | bytes 9175296 | tf_op jit(solution)/shard_map/efij,efrj->eri/dot_general | solution.py:80
  113.7 8.1 %collective-permute-start.19 = (bf16[16,8,128]{2,1,0:T(8,128)(2,1)S(1)}, bf16[16,8,128]{2,1,0:T(8,128)(2,1)S(1)}, u32[]{:S(2)}, u32[]{:S(2)}) collective-permute-start(bf16[16,8,128]{2,1,0:T(8,128)(2,1)S(1)} %get-tuple-element.35), channel_id=1, source_target_pairs={{1,0},{2,1},{3,2},{4,3},{5,4},{6,5},{7,6},{8,7},{9,8},{10,9},{11,1... | collective-permute-start | bytes 98312 | tf_op jit(solution)/shard_map/ppermute | solution.py:13
  123.7 9.5 %collective-permute-start.21 = (bf16[16,8,128]{2,1,0:T(8,128)(2,1)S(1)}, bf16[16,8,128]{2,1,0:T(8,128)(2,1)S(1)}, u32[]{:S(2)}, u32[]{:S(2)}) collective-permute-start(bf16[16,8,128]{2,1,0:T(8,128)(2,1)S(1)} %get-tuple-element.33), channel_id=1, source_target_pairs={{0,15},{1,16},{2,17},{3,18},{4,19},{5,20},{6,21},{7,22},{8,23},{9,... | collective-permute-start | bytes 98312 | tf_op jit(solution)/shard_map/ppermute | solution.py:13
  133.3 7.8 %collective-permute-start.22 = (bf16[16,8,128]{2,1,0:T(8,128)(2,1)S(1)}, bf16[16,8,128]{2,1,0:T(8,128)(2,1)S(1)}, u32[]{:S(2)}, u32[]{:S(2)}) collective-permute-start(bf16[16,8,128]{2,1,0:T(8,128)(2,1)S(1)} %get-tuple-element.32), channel_id=1, source_target_pairs={{0,16},{1,17},{2,18},{3,19},{4,20},{5,21},{6,22},{7,23},{8,24},{9,... | collective-permute-start | bytes 98312 | tf_op jit(solution)/shard_map/ppermute | solution.py:13
  144.3 2.6 gather_fusion.5
  146.9 5.9 %convolution_bitcast_fusion.1 = f32[64,8,128]{2,1,0:T(8,128)S(1)} fusion(bf16[64,4,128,128]{3,2,1,0:T(8,128)(2,1)} %param.8, bf16[64,4,8,128]{3,2,1,0:T(8,128)(2,1)} %bitcast.297, pred[64,4]{1,0:T(8,128)(4,1)S(1)} %copy.36), kind=kOutput, calls=%fused_computation.14 | convolution fusion | flops 67371008 | bytes 9175296 | tf_op jit(solution)/shard_map/efij,efrj->eri/dot_general | solution.py:80
  161.0 1.9 collective-permute-start.26
  162.9 8.2 %collective-permute-start.27 = (bf16[16,8,128]{2,1,0:T(8,128)(2,1)S(1)}, bf16[16,8,128]{2,1,0:T(8,128)(2,1)S(1)}, u32[]{:S(2)}, u32[]{:S(2)}) collective-permute-start(bf16[16,8,128]{2,1,0:T(8,128)(2,1)S(1)} %get-tuple-element.27), channel_id=1, source_target_pairs={{1,0},{2,1},{3,2},{4,3},{5,4},{6,5},{7,6},{8,7},{9,8},{10,9},{11,1... | collective-permute-start | bytes 98312 | tf_op jit(solution)/shard_map/ppermute | solution.py:13
  171.1 1.9 collective-permute-start.28
  173.0 9.6 %collective-permute-start.29 = (bf16[16,8,128]{2,1,0:T(8,128)(2,1)S(1)}, bf16[16,8,128]{2,1,0:T(8,128)(2,1)S(1)}, u32[]{:S(2)}, u32[]{:S(2)}) collective-permute-start(bf16[16,8,128]{2,1,0:T(8,128)(2,1)S(1)} %get-tuple-element.25), channel_id=1, source_target_pairs={{0,15},{1,16},{2,17},{3,18},{4,19},{5,20},{6,21},{7,22},{8,23},{9,... | collective-permute-start | bytes 98312 | tf_op jit(solution)/shard_map/ppermute | solution.py:13
  182.7 7.8 %collective-permute-start.30 = (bf16[16,8,128]{2,1,0:T(8,128)(2,1)S(1)}, bf16[16,8,128]{2,1,0:T(8,128)(2,1)S(1)}, u32[]{:S(2)}, u32[]{:S(2)}) collective-permute-start(bf16[16,8,128]{2,1,0:T(8,128)(2,1)S(1)} %get-tuple-element.24), channel_id=1, source_target_pairs={{0,16},{1,17},{2,18},{3,19},{4,20},{5,21},{6,22},{7,23},{8,24},{9,... | collective-permute-start | bytes 98312 | tf_op jit(solution)/shard_map/ppermute | solution.py:13
  193.6 2.6 gather_fusion.7
  196.2 5.9 %convolution_bitcast_fusion = f32[64,8,128]{2,1,0:T(8,128)S(1)} fusion(bf16[64,4,128,128]{3,2,1,0:T(8,128)(2,1)} %param.8, bf16[64,4,8,128]{3,2,1,0:T(8,128)(2,1)} %bitcast.294, pred[64,4]{1,0:T(8,128)(4,1)S(1)} %copy.36), kind=kOutput, calls=%fused_computation.10 | convolution fusion | flops 67371008 | bytes 9175296 | tf_op jit(solution)/shard_map/efij,efrj->eri/dot_general | solution.py:80
  204.0 4.9 %fusion.7 = f32[8,5,5]{1,2,0:T(8,128)S(1)} fusion(f32[5,64,8,128]{3,2,1,0:T(8,128)S(1)} %get-tuple-element.61), kind=kOutput, calls=%fused_computation.23 | convolution fusion | flops 19660800 | bytes 1311520 | tf_op jit(solution)/shard_map/icrn,jcrn->rij/dot_general | solution.py:85
  209.0 87.5 %psum.7 = f32[8,5,5]{1,2,0:T(8,128)S(1)} all-reduce(f32[8,5,5]{1,2,0:T(8,128)S(1)} %fusion.7), channel_id=1, replica_groups=mesh['gx'=16,'gy'=16] {'gx','gy'}, use_global_device_ids=true, to_apply=%region_0.1 | all-reduce | flops 200 | bytes 1600 | tf_op jit(solution)/shard_map/psum | solution.py:86
  296.9 3.0 custom-call.4
  302.3 2.5 fusion.12
  305.7 2.5 fusion.10
  (164 shorter events, 58.4 us)
Async XLA Ops:
  6.6 19.6 %collective-permute-start = (bf16[16,8,128]{2,1,0:T(8,128)(2,1)}, bf16[16,8,128]{2,1,0:T(8,128)(2,1)}, u32[]{:S(2)}, u32[]{:S(2)}) collective-permute-start(bf16[16,8,128]{2,1,0:T(8,128)(2,1)} %get-tuple-element.54), channel_id=1, source_target_pairs={{17,0},{18,1},{19,2},{20,3},{21,4},{22,5},{23,6},{24,7},{25,8},{26... | collective-permute-start | bytes 98312 | tf_op jit(solution)/shard_map/ppermute | solution.py:13
  7.9 27.4 %collective-permute-start.1 = (bf16[16,8,128]{2,1,0:T(8,128)(2,1)}, bf16[16,8,128]{2,1,0:T(8,128)(2,1)}, u32[]{:S(2)}, u32[]{:S(2)}) collective-permute-start(bf16[16,8,128]{2,1,0:T(8,128)(2,1)} %get-tuple-element.53), channel_id=1, source_target_pairs={{16,0},{17,1},{18,2},{19,3},{20,4},{21,5},{22,6},{23,7},{24,8},{25... | collective-permute-start | bytes 98312 | tf_op jit(solution)/shard_map/ppermute | solution.py:13
  13.1 29.8 %collective-permute-start.2 = (bf16[16,8,128]{2,1,0:T(8,128)(2,1)}, bf16[16,8,128]{2,1,0:T(8,128)(2,1)}, u32[]{:S(2)}, u32[]{:S(2)}) collective-permute-start(bf16[16,8,128]{2,1,0:T(8,128)(2,1)} %get-tuple-element.52), channel_id=1, source_target_pairs={{15,0},{16,1},{17,2},{18,3},{19,4},{20,5},{21,6},{22,7},{23,8},{24... | collective-permute-start | bytes 98312 | tf_op jit(solution)/shard_map/ppermute | solution.py:13
  15.0 29.2 %collective-permute-start.3 = (bf16[16,8,128]{2,1,0:T(8,128)(2,1)}, bf16[16,8,128]{2,1,0:T(8,128)(2,1)}, u32[]{:S(2)}, u32[]{:S(2)}) collective-permute-start(bf16[16,8,128]{2,1,0:T(8,128)(2,1)} %get-tuple-element.51), channel_id=1, source_target_pairs={{1,0},{2,1},{3,2},{4,3},{5,4},{6,5},{7,6},{8,7},{9,8},{10,9},{11,1... | collective-permute-start | bytes 98312 | tf_op jit(solution)/shard_map/ppermute | solution.py:13
  21.2 23.8 %collective-permute-start.4 = (bf16[16,8,128]{2,1,0:T(8,128)(2,1)}, bf16[16,8,128]{2,1,0:T(8,128)(2,1)}, u32[]{:S(2)}, u32[]{:S(2)}) collective-permute-start(bf16[16,8,128]{2,1,0:T(8,128)(2,1)} %get-tuple-element.50), channel_id=1, source_target_pairs={{0,1},{1,2},{2,3},{3,4},{4,5},{5,6},{6,7},{7,8},{8,9},{9,10},{10,1... | collective-permute-start | bytes 98312 | tf_op jit(solution)/shard_map/ppermute | solution.py:13
  26.2 18.8 %collective-permute-start.5 = (bf16[16,8,128]{2,1,0:T(8,128)(2,1)}, bf16[16,8,128]{2,1,0:T(8,128)(2,1)S(1)}, u32[]{:S(2)}, u32[]{:S(2)}) collective-permute-start(bf16[16,8,128]{2,1,0:T(8,128)(2,1)} %get-tuple-element.49), channel_id=1, source_target_pairs={{0,15},{1,16},{2,17},{3,18},{4,19},{5,20},{6,21},{7,22},{8,23},{9,... | collective-permute-start | bytes 98312 | tf_op jit(solution)/shard_map/ppermute | solution.py:13
  35.3 9.8 %collective-permute-start.6 = (bf16[16,8,128]{2,1,0:T(8,128)(2,1)}, bf16[16,8,128]{2,1,0:T(8,128)(2,1)S(1)}, u32[]{:S(2)}, u32[]{:S(2)}) collective-permute-start(bf16[16,8,128]{2,1,0:T(8,128)(2,1)} %get-tuple-element.48), channel_id=1, source_target_pairs={{0,16},{1,17},{2,18},{3,19},{4,20},{5,21},{6,22},{7,23},{8,24},{9,... | collective-permute-start | bytes 98312 | tf_op jit(solution)/shard_map/ppermute | solution.py:13
  42.9 2.6 collective-permute-start.7
  59.4 15.2 %collective-permute-start.8 = (bf16[16,8,128]{2,1,0:T(8,128)(2,1)S(1)}, bf16[16,8,128]{2,1,0:T(8,128)(2,1)S(1)}, u32[]{:S(2)}, u32[]{:S(2)}) collective-permute-start(bf16[16,8,128]{2,1,0:T(8,128)(2,1)S(1)} %get-tuple-element.46), channel_id=1, source_target_pairs={{17,0},{18,1},{19,2},{20,3},{21,4},{22,5},{23,6},{24,7},{25,8},{26... | collective-permute-start | bytes 98312 | tf_op jit(solution)/shard_map/ppermute | solution.py:13
  60.7 23.4 %collective-permute-start.9 = (bf16[16,8,128]{2,1,0:T(8,128)(2,1)S(1)}, bf16[16,8,128]{2,1,0:T(8,128)(2,1)S(1)}, u32[]{:S(2)}, u32[]{:S(2)}) collective-permute-start(bf16[16,8,128]{2,1,0:T(8,128)(2,1)S(1)} %get-tuple-element.45), channel_id=1, source_target_pairs={{16,0},{17,1},{18,2},{19,3},{20,4},{21,5},{22,6},{23,7},{24,8},{25... | collective-permute-start | bytes 98312 | tf_op jit(solution)/shard_map/ppermute | solution.py:13
  62.6 29.3 %collective-permute-start.10 = (bf16[16,8,128]{2,1,0:T(8,128)(2,1)S(1)}, bf16[16,8,128]{2,1,0:T(8,128)(2,1)S(1)}, u32[]{:S(2)}, u32[]{:S(2)}) collective-permute-start(bf16[16,8,128]{2,1,0:T(8,128)(2,1)S(1)} %get-tuple-element.44), channel_id=1, source_target_pairs={{15,0},{16,1},{17,2},{18,3},{19,4},{20,5},{21,6},{22,7},{23,8},{24... | collective-permute-start | bytes 98312 | tf_op jit(solution)/shard_map/ppermute | solution.py:13
  64.5 28.7 %collective-permute-start.11 = (bf16[16,8,128]{2,1,0:T(8,128)(2,1)S(1)}, bf16[16,8,128]{2,1,0:T(8,128)(2,1)S(1)}, u32[]{:S(2)}, u32[]{:S(2)}) collective-permute-start(bf16[16,8,128]{2,1,0:T(8,128)(2,1)S(1)} %get-tuple-element.43), channel_id=1, source_target_pairs={{1,0},{2,1},{3,2},{4,3},{5,4},{6,5},{7,6},{8,7},{9,8},{10,9},{11,1... | collective-permute-start | bytes 98312 | tf_op jit(solution)/shard_map/ppermute | solution.py:13
  72.6 20.6 %collective-permute-start.12 = (bf16[16,8,128]{2,1,0:T(8,128)(2,1)S(1)}, bf16[16,8,128]{2,1,0:T(8,128)(2,1)S(1)}, u32[]{:S(2)}, u32[]{:S(2)}) collective-permute-start(bf16[16,8,128]{2,1,0:T(8,128)(2,1)S(1)} %get-tuple-element.42), channel_id=1, source_target_pairs={{0,1},{1,2},{2,3},{3,4},{4,5},{5,6},{6,7},{7,8},{8,9},{9,10},{10,1... | collective-permute-start | bytes 98312 | tf_op jit(solution)/shard_map/ppermute | solution.py:13
  74.5 18.7 %collective-permute-start.13 = (bf16[16,8,128]{2,1,0:T(8,128)(2,1)S(1)}, bf16[16,8,128]{2,1,0:T(8,128)(2,1)S(1)}, u32[]{:S(2)}, u32[]{:S(2)}) collective-permute-start(bf16[16,8,128]{2,1,0:T(8,128)(2,1)S(1)} %get-tuple-element.41), channel_id=1, source_target_pairs={{0,15},{1,16},{2,17},{3,18},{4,19},{5,20},{6,21},{7,22},{8,23},{9,... | collective-permute-start | bytes 98312 | tf_op jit(solution)/shard_map/ppermute | solution.py:13
  84.1 9.2 %collective-permute-start.14 = (bf16[16,8,128]{2,1,0:T(8,128)(2,1)S(1)}, bf16[16,8,128]{2,1,0:T(8,128)(2,1)S(1)}, u32[]{:S(2)}, u32[]{:S(2)}) collective-permute-start(bf16[16,8,128]{2,1,0:T(8,128)(2,1)S(1)} %get-tuple-element.40), channel_id=1, source_target_pairs={{0,16},{1,17},{2,18},{3,19},{4,20},{5,21},{6,22},{7,23},{8,24},{9,... | collective-permute-start | bytes 98312 | tf_op jit(solution)/shard_map/ppermute | solution.py:13
  91.9 2.3 collective-permute-start.15
  108.0 15.7 %collective-permute-start.16 = (bf16[16,8,128]{2,1,0:T(8,128)(2,1)S(1)}, bf16[16,8,128]{2,1,0:T(8,128)(2,1)S(1)}, u32[]{:S(2)}, u32[]{:S(2)}) collective-permute-start(bf16[16,8,128]{2,1,0:T(8,128)(2,1)S(1)} %get-tuple-element.38), channel_id=1, source_target_pairs={{17,0},{18,1},{19,2},{20,3},{21,4},{22,5},{23,6},{24,7},{25,8},{26... | collective-permute-start | bytes 98312 | tf_op jit(solution)/shard_map/ppermute | solution.py:13
  109.8 23.4 %collective-permute-start.17 = (bf16[16,8,128]{2,1,0:T(8,128)(2,1)S(1)}, bf16[16,8,128]{2,1,0:T(8,128)(2,1)S(1)}, u32[]{:S(2)}, u32[]{:S(2)}) collective-permute-start(bf16[16,8,128]{2,1,0:T(8,128)(2,1)S(1)} %get-tuple-element.37), channel_id=1, source_target_pairs={{16,0},{17,1},{18,2},{19,3},{20,4},{21,5},{22,6},{23,7},{24,8},{25... | collective-permute-start | bytes 98312 | tf_op jit(solution)/shard_map/ppermute | solution.py:13
  111.8 29.4 %collective-permute-start.18 = (bf16[16,8,128]{2,1,0:T(8,128)(2,1)S(1)}, bf16[16,8,128]{2,1,0:T(8,128)(2,1)S(1)}, u32[]{:S(2)}, u32[]{:S(2)}) collective-permute-start(bf16[16,8,128]{2,1,0:T(8,128)(2,1)S(1)} %get-tuple-element.36), channel_id=1, source_target_pairs={{15,0},{16,1},{17,2},{18,3},{19,4},{20,5},{21,6},{22,7},{23,8},{24... | collective-permute-start | bytes 98312 | tf_op jit(solution)/shard_map/ppermute | solution.py:13
  113.7 28.8 %collective-permute-start.19 = (bf16[16,8,128]{2,1,0:T(8,128)(2,1)S(1)}, bf16[16,8,128]{2,1,0:T(8,128)(2,1)S(1)}, u32[]{:S(2)}, u32[]{:S(2)}) collective-permute-start(bf16[16,8,128]{2,1,0:T(8,128)(2,1)S(1)} %get-tuple-element.35), channel_id=1, source_target_pairs={{1,0},{2,1},{3,2},{4,3},{5,4},{6,5},{7,6},{8,7},{9,8},{10,9},{11,1... | collective-permute-start | bytes 98312 | tf_op jit(solution)/shard_map/ppermute | solution.py:13
  121.8 20.7 %collective-permute-start.20 = (bf16[16,8,128]{2,1,0:T(8,128)(2,1)S(1)}, bf16[16,8,128]{2,1,0:T(8,128)(2,1)S(1)}, u32[]{:S(2)}, u32[]{:S(2)}) collective-permute-start(bf16[16,8,128]{2,1,0:T(8,128)(2,1)S(1)} %get-tuple-element.34), channel_id=1, source_target_pairs={{0,1},{1,2},{2,3},{3,4},{4,5},{5,6},{6,7},{7,8},{8,9},{9,10},{10,1... | collective-permute-start | bytes 98312 | tf_op jit(solution)/shard_map/ppermute | solution.py:13
  123.7 18.8 %collective-permute-start.21 = (bf16[16,8,128]{2,1,0:T(8,128)(2,1)S(1)}, bf16[16,8,128]{2,1,0:T(8,128)(2,1)S(1)}, u32[]{:S(2)}, u32[]{:S(2)}) collective-permute-start(bf16[16,8,128]{2,1,0:T(8,128)(2,1)S(1)} %get-tuple-element.33), channel_id=1, source_target_pairs={{0,15},{1,16},{2,17},{3,18},{4,19},{5,20},{6,21},{7,22},{8,23},{9,... | collective-permute-start | bytes 98312 | tf_op jit(solution)/shard_map/ppermute | solution.py:13
  133.3 9.3 %collective-permute-start.22 = (bf16[16,8,128]{2,1,0:T(8,128)(2,1)S(1)}, bf16[16,8,128]{2,1,0:T(8,128)(2,1)S(1)}, u32[]{:S(2)}, u32[]{:S(2)}) collective-permute-start(bf16[16,8,128]{2,1,0:T(8,128)(2,1)S(1)} %get-tuple-element.32), channel_id=1, source_target_pairs={{0,16},{1,17},{2,18},{3,19},{4,20},{5,21},{6,22},{7,23},{8,24},{9,... | collective-permute-start | bytes 98312 | tf_op jit(solution)/shard_map/ppermute | solution.py:13
  141.1 2.3 collective-permute-start.23
  157.3 15.7 %collective-permute-start.24 = (bf16[16,8,128]{2,1,0:T(8,128)(2,1)S(1)}, bf16[16,8,128]{2,1,0:T(8,128)(2,1)S(1)}, u32[]{:S(2)}, u32[]{:S(2)}) collective-permute-start(bf16[16,8,128]{2,1,0:T(8,128)(2,1)S(1)} %get-tuple-element.30), channel_id=1, source_target_pairs={{17,0},{18,1},{19,2},{20,3},{21,4},{22,5},{23,6},{24,7},{25,8},{26... | collective-permute-start | bytes 98312 | tf_op jit(solution)/shard_map/ppermute | solution.py:13
  159.1 23.6 %collective-permute-start.25 = (bf16[16,8,128]{2,1,0:T(8,128)(2,1)S(1)}, bf16[16,8,128]{2,1,0:T(8,128)(2,1)S(1)}, u32[]{:S(2)}, u32[]{:S(2)}) collective-permute-start(bf16[16,8,128]{2,1,0:T(8,128)(2,1)S(1)} %get-tuple-element.29), channel_id=1, source_target_pairs={{16,0},{17,1},{18,2},{19,3},{20,4},{21,5},{22,6},{23,7},{24,8},{25... | collective-permute-start | bytes 98312 | tf_op jit(solution)/shard_map/ppermute | solution.py:13
  161.0 29.5 %collective-permute-start.26 = (bf16[16,8,128]{2,1,0:T(8,128)(2,1)S(1)}, bf16[16,8,128]{2,1,0:T(8,128)(2,1)S(1)}, u32[]{:S(2)}, u32[]{:S(2)}) collective-permute-start(bf16[16,8,128]{2,1,0:T(8,128)(2,1)S(1)} %get-tuple-element.28), channel_id=1, source_target_pairs={{15,0},{16,1},{17,2},{18,3},{19,4},{20,5},{21,6},{22,7},{23,8},{24... | collective-permute-start | bytes 98312 | tf_op jit(solution)/shard_map/ppermute | solution.py:13
  162.9 29.1 %collective-permute-start.27 = (bf16[16,8,128]{2,1,0:T(8,128)(2,1)S(1)}, bf16[16,8,128]{2,1,0:T(8,128)(2,1)S(1)}, u32[]{:S(2)}, u32[]{:S(2)}) collective-permute-start(bf16[16,8,128]{2,1,0:T(8,128)(2,1)S(1)} %get-tuple-element.27), channel_id=1, source_target_pairs={{1,0},{2,1},{3,2},{4,3},{5,4},{6,5},{7,6},{8,7},{9,8},{10,9},{11,1... | collective-permute-start | bytes 98312 | tf_op jit(solution)/shard_map/ppermute | solution.py:13
  171.1 21.0 %collective-permute-start.28 = (bf16[16,8,128]{2,1,0:T(8,128)(2,1)S(1)}, bf16[16,8,128]{2,1,0:T(8,128)(2,1)S(1)}, u32[]{:S(2)}, u32[]{:S(2)}) collective-permute-start(bf16[16,8,128]{2,1,0:T(8,128)(2,1)S(1)} %get-tuple-element.26), channel_id=1, source_target_pairs={{0,1},{1,2},{2,3},{3,4},{4,5},{5,6},{6,7},{7,8},{8,9},{9,10},{10,1... | collective-permute-start | bytes 98312 | tf_op jit(solution)/shard_map/ppermute | solution.py:13
  173.0 19.0 %collective-permute-start.29 = (bf16[16,8,128]{2,1,0:T(8,128)(2,1)S(1)}, bf16[16,8,128]{2,1,0:T(8,128)(2,1)S(1)}, u32[]{:S(2)}, u32[]{:S(2)}) collective-permute-start(bf16[16,8,128]{2,1,0:T(8,128)(2,1)S(1)} %get-tuple-element.25), channel_id=1, source_target_pairs={{0,15},{1,16},{2,17},{3,18},{4,19},{5,20},{6,21},{7,22},{8,23},{9,... | collective-permute-start | bytes 98312 | tf_op jit(solution)/shard_map/ppermute | solution.py:13
  182.7 9.5 %collective-permute-start.30 = (bf16[16,8,128]{2,1,0:T(8,128)(2,1)S(1)}, bf16[16,8,128]{2,1,0:T(8,128)(2,1)S(1)}, u32[]{:S(2)}, u32[]{:S(2)}) collective-permute-start(bf16[16,8,128]{2,1,0:T(8,128)(2,1)S(1)} %get-tuple-element.24), channel_id=1, source_target_pairs={{0,16},{1,17},{2,18},{3,19},{4,20},{5,21},{6,22},{7,23},{8,24},{9,... | collective-permute-start | bytes 98312 | tf_op jit(solution)/shard_map/ppermute | solution.py:13
  190.5 2.3 collective-permute-start.31
  (14 other events, 341.8 us)
where the time goes:
time: 311 us; the launch traced here: 309 us
  starting transfers between devices  134 us (43%)
  blocking collectives  87.5 us (28%)
  matrix products  38.9 us (13%)
  other arithmetic  22.7 us (7%)
  local copies, waits for them, and re-layouts  20.8 us (7%)
    ppermute x32, starting transfers between devices, passed_along(): return lax.ppermute(block, axis, route)  134 us
    psum x1, blocking collectives, per_device(): gram = lax.psum(local_gram, ('gx', 'gy'))  87.5 us
    dot_general x4, matrix products, per_device(): jnp.einsum('efij,efrj->eri', face_blocks, gathered, preferred_element_typ...  23.5 us
    gather x4, local copies, waits for them, and re-layouts, per_device(): gathered = jnp.where(present[:, :, None, None], lookup[source], zero_half)  10.4 us
  transfers between devices with their start and end apart: 32, of which 4 were waited for; matrix products, arithmetic and copies ran while one was open for 2% of the time, Pallas kernels for 0%

commit v1 on v0

--- a/solution.py
+++ b/solution.py
@@ -2,6 +2,7 @@
 import jax.numpy as jnp
 from jax import lax
 from jax.sharding import PartitionSpec as P
+from jax.lax import psum
 
 POWERS = 4
 HIGH = lax.Precision.HIGHEST
@@ -83,7 +84,15 @@
         vectors.append((own_part + face_part) * live_mask)
     basis = jnp.stack(vectors)
     local_gram = jnp.einsum("icrn,jcrn->rij", basis, basis, precision=HIGH)
-    gram = lax.psum(local_gram, ("gx", "gy"))
+
+    def manage_the_core(inp):
+        dev_axis = "gx"
+        axis_id = "gy"
+        for j0 in (dev_axis, axis_id):
+            inp = psum(inp, j0)
+        return inp
+
+    gram = manage_the_core(local_gram)
     weights = coefficients(gram)
     solution = jnp.einsum("rk,kcrn->crn", weights, basis[:POWERS], precision=HIGH)
     residual = basis[0] - jnp.einsum("rk,kcrn->crn", weights, basis[1:], precision=HIGH)

time: 311 us -> 350 us (1.13)
  the two profiles are of different devices: /device:TPU:1 before, /device:TPU:128 now
where the time goes in v1:
time: 350 us; the launch traced here: 348 us
  blocking collectives  116 us (33%)
  starting transfers between devices  111 us (32%)
  matrix products  38.9 us (11%)
  waiting for transfers between devices  36.9 us (11%)
  other arithmetic  22.7 us (6%)
  local copies, waits for them, and re-layouts  20.6 us (6%)
    psum x2, blocking collectives, manage_the_core(): inp = psum(inp, j0)  116 us
    ppermute x32, starting transfers between devices, passed_along(): return lax.ppermute(block, axis, route)  111 us
    ppermute x32, waiting for transfers between devices, passed_along(): return lax.ppermute(block, axis, route)  36.9 us
    dot_general x4, matrix products, per_device(): jnp.einsum('efij,efrj->eri', face_blocks, gathered, preferred_element_typ...  23.5 us
    gather x4, local copies, waits for them, and re-layouts, per_device(): gathered = jnp.where(present[:, :, None, None], lookup[source], zero_half)  10.3 us
  transfers between devices with their start and end apart: 32, of which 8 were waited for; matrix products, arithmetic and copies ran while one was open for 2% of the time, Pallas kernels for 0%

profile of v1, /device:TPU:128, one launch (start us, length us, event | category | flops | bytes accessed | tf_op | source)
XLA Modules:
  0.0 347.8 jit_solution(17466798394831512470)
XLA Ops:
  6.6 6.7 %collective-permute-start = (bf16[16,8,128]{2,1,0:T(8,128)(2,1)}, bf16[16,8,128]{2,1,0:T(8,128)(2,1)}, u32[]{:S(2)}, u32[]{:S(2)}) collective-permute-start(bf16[16,8,128]{2,1,0:T(8,128)(2,1)} %get-tuple-element.54), channel_id=1, source_target_pairs={{17,0},{18,1},{19,2},{20,3},{21,4},{22,5},{23,6},{24,7},{25,8},{26... | collective-permute-start | bytes 98312 | tf_op jit(solution)/shard_map/ppermute | solution.py:14
  17.1 6.6 %collective-permute-start.3 = (bf16[16,8,128]{2,1,0:T(8,128)(2,1)}, bf16[16,8,128]{2,1,0:T(8,128)(2,1)}, u32[]{:S(2)}, u32[]{:S(2)}) collective-permute-start(bf16[16,8,128]{2,1,0:T(8,128)(2,1)} %get-tuple-element.51), channel_id=1, source_target_pairs={{1,0},{2,1},{3,2},{4,3},{5,4},{6,5},{7,6},{8,7},{9,8},{10,9},{11,1... | collective-permute-start | bytes 98312 | tf_op jit(solution)/shard_map/ppermute | solution.py:14
  28.7 7.6 %collective-permute-start.5 = (bf16[16,8,128]{2,1,0:T(8,128)(2,1)}, bf16[16,8,128]{2,1,0:T(8,128)(2,1)S(1)}, u32[]{:S(2)}, u32[]{:S(2)}) collective-permute-start(bf16[16,8,128]{2,1,0:T(8,128)(2,1)} %get-tuple-element.49), channel_id=1, source_target_pairs={{0,15},{1,16},{2,17},{3,18},{4,19},{5,20},{6,21},{7,22},{8,23},{9,... | collective-permute-start | bytes 98312 | tf_op jit(solution)/shard_map/ppermute | solution.py:14
  37.1 2.7 collective-permute-start.6
  43.8 8.4 %collective-permute-done.7 = bf16[16,8,128]{2,1,0:T(8,128)(2,1)S(1)} collective-permute-done((bf16[16,8,128]{2,1,0:T(8,128)(2,1)}, bf16[16,8,128]{2,1,0:T(8,128)(2,1)S(1)}, u32[]{:S(2)}, u32[]{:S(2)}) %collective-permute-start.7) | collective-permute-done | bytes 32800 | tf_op jit(solution)/shard_map/ppermute | solution.py:14
  53.0 2.6 gather_fusion.1
  55.6 5.9 %convolution_bitcast_fusion.3 = f32[64,8,128]{2,1,0:T(8,128)S(1)} fusion(bf16[64,4,128,128]{3,2,1,0:T(8,128)(2,1)} %param.8, bf16[64,4,8,128]{3,2,1,0:T(8,128)(2,1)} %bitcast.295, pred[64,4]{1,0:T(8,128)(4,1)S(1)} %copy.36), kind=kOutput, calls=%fused_computation.20 | convolution fusion | flops 67371008 | bytes 9175296 | tf_op jit(solution)/shard_map/efij,efrj->eri/dot_general | solution.py:81
  69.9 3.2 collective-permute-start.10
  73.1 5.3 %collective-permute-start.11 = (bf16[16,8,128]{2,1,0:T(8,128)(2,1)S(1)}, bf16[16,8,128]{2,1,0:T(8,128)(2,1)S(1)}, u32[]{:S(2)}, u32[]{:S(2)}) collective-permute-start(bf16[16,8,128]{2,1,0:T(8,128)(2,1)S(1)} %get-tuple-element.43), channel_id=1, source_target_pairs={{1,0},{2,1},{3,2},{4,3},{5,4},{6,5},{7,6},{8,7},{9,8},{10,9},{11,1... | collective-permute-start | bytes 98312 | tf_op jit(solution)/shard_map/ppermute | solution.py:14
  80.4 7.6 %collective-permute-start.13 = (bf16[16,8,128]{2,1,0:T(8,128)(2,1)S(1)}, bf16[16,8,128]{2,1,0:T(8,128)(2,1)S(1)}, u32[]{:S(2)}, u32[]{:S(2)}) collective-permute-start(bf16[16,8,128]{2,1,0:T(8,128)(2,1)S(1)} %get-tuple-element.41), channel_id=1, source_target_pairs={{0,15},{1,16},{2,17},{3,18},{4,19},{5,20},{6,21},{7,22},{8,23},{9,... | collective-permute-start | bytes 98312 | tf_op jit(solution)/shard_map/ppermute | solution.py:14
  88.0 2.7 collective-permute-start.14
  94.5 7.8 %collective-permute-done.15 = bf16[16,8,128]{2,1,0:T(8,128)(2,1)S(1)} collective-permute-done((bf16[16,8,128]{2,1,0:T(8,128)(2,1)S(1)}, bf16[16,8,128]{2,1,0:T(8,128)(2,1)S(1)}, u32[]{:S(2)}, u32[]{:S(2)}) %collective-permute-start.15) | collective-permute-done | bytes 32800 | tf_op jit(solution)/shard_map/ppermute | solution.py:14
  103.1 2.6 gather_fusion.3
  105.7 5.9 %convolution_bitcast_fusion.2 = f32[64,8,128]{2,1,0:T(8,128)S(1)} fusion(bf16[64,4,128,128]{3,2,1,0:T(8,128)(2,1)} %param.8, bf16[64,4,8,128]{3,2,1,0:T(8,128)(2,1)} %bitcast.296, pred[64,4]{1,0:T(8,128)(4,1)S(1)} %copy.36), kind=kOutput, calls=%fused_computation.17 | convolution fusion | flops 67371008 | bytes 9175296 | tf_op jit(solution)/shard_map/efij,efrj->eri/dot_general | solution.py:81
  120.6 3.0 collective-permute-start.18
  123.6 5.3 %collective-permute-start.19 = (bf16[16,8,128]{2,1,0:T(8,128)(2,1)S(1)}, bf16[16,8,128]{2,1,0:T(8,128)(2,1)S(1)}, u32[]{:S(2)}, u32[]{:S(2)}) collective-permute-start(bf16[16,8,128]{2,1,0:T(8,128)(2,1)S(1)} %get-tuple-element.35), channel_id=1, source_target_pairs={{1,0},{2,1},{3,2},{4,3},{5,4},{6,5},{7,6},{8,7},{9,8},{10,9},{11,1... | collective-permute-start | bytes 98312 | tf_op jit(solution)/shard_map/ppermute | solution.py:14
  130.9 7.7 %collective-permute-start.21 = (bf16[16,8,128]{2,1,0:T(8,128)(2,1)S(1)}, bf16[16,8,128]{2,1,0:T(8,128)(2,1)S(1)}, u32[]{:S(2)}, u32[]{:S(2)}) collective-permute-start(bf16[16,8,128]{2,1,0:T(8,128)(2,1)S(1)} %get-tuple-element.33), channel_id=1, source_target_pairs={{0,15},{1,16},{2,17},{3,18},{4,19},{5,20},{6,21},{7,22},{8,23},{9,... | collective-permute-start | bytes 98312 | tf_op jit(solution)/shard_map/ppermute | solution.py:14
  138.7 2.7 collective-permute-start.22
  145.1 7.9 %collective-permute-done.23 = bf16[16,8,128]{2,1,0:T(8,128)(2,1)S(1)} collective-permute-done((bf16[16,8,128]{2,1,0:T(8,128)(2,1)S(1)}, bf16[16,8,128]{2,1,0:T(8,128)(2,1)S(1)}, u32[]{:S(2)}, u32[]{:S(2)}) %collective-permute-start.23) | collective-permute-done | bytes 32800 | tf_op jit(solution)/shard_map/ppermute | solution.py:14
  153.8 2.6 gather_fusion.5
  156.4 5.9 %convolution_bitcast_fusion.1 = f32[64,8,128]{2,1,0:T(8,128)S(1)} fusion(bf16[64,4,128,128]{3,2,1,0:T(8,128)(2,1)} %param.8, bf16[64,4,8,128]{3,2,1,0:T(8,128)(2,1)} %bitcast.297, pred[64,4]{1,0:T(8,128)(4,1)S(1)} %copy.36), kind=kOutput, calls=%fused_computation.14 | convolution fusion | flops 67371008 | bytes 9175296 | tf_op jit(solution)/shard_map/efij,efrj->eri/dot_general | solution.py:81
  171.2 2.7 collective-permute-start.26
  173.9 5.3 %collective-permute-start.27 = (bf16[16,8,128]{2,1,0:T(8,128)(2,1)S(1)}, bf16[16,8,128]{2,1,0:T(8,128)(2,1)S(1)}, u32[]{:S(2)}, u32[]{:S(2)}) collective-permute-start(bf16[16,8,128]{2,1,0:T(8,128)(2,1)S(1)} %get-tuple-element.27), channel_id=1, source_target_pairs={{1,0},{2,1},{3,2},{4,3},{5,4},{6,5},{7,6},{8,7},{9,8},{10,9},{11,1... | collective-permute-start | bytes 98312 | tf_op jit(solution)/shard_map/ppermute | solution.py:14
  181.2 8.1 %collective-permute-start.29 = (bf16[16,8,128]{2,1,0:T(8,128)(2,1)S(1)}, bf16[16,8,128]{2,1,0:T(8,128)(2,1)S(1)}, u32[]{:S(2)}, u32[]{:S(2)}) collective-permute-start(bf16[16,8,128]{2,1,0:T(8,128)(2,1)S(1)} %get-tuple-element.25), channel_id=1, source_target_pairs={{0,15},{1,16},{2,17},{3,18},{4,19},{5,20},{6,21},{7,22},{8,23},{9,... | collective-permute-start | bytes 98312 | tf_op jit(solution)/shard_map/ppermute | solution.py:14
  189.3 2.7 collective-permute-start.30
  195.8 7.9 %collective-permute-done.31 = bf16[16,8,128]{2,1,0:T(8,128)(2,1)S(1)} collective-permute-done((bf16[16,8,128]{2,1,0:T(8,128)(2,1)S(1)}, bf16[16,8,128]{2,1,0:T(8,128)(2,1)S(1)}, u32[]{:S(2)}, u32[]{:S(2)}) %collective-permute-start.31) | collective-permute-done | bytes 32800 | tf_op jit(solution)/shard_map/ppermute | solution.py:14
  204.4 2.6 gather_fusion.7
  207.0 5.9 %convolution_bitcast_fusion = f32[64,8,128]{2,1,0:T(8,128)S(1)} fusion(bf16[64,4,128,128]{3,2,1,0:T(8,128)(2,1)} %param.8, bf16[64,4,8,128]{3,2,1,0:T(8,128)(2,1)} %bitcast.294, pred[64,4]{1,0:T(8,128)(4,1)S(1)} %copy.36), kind=kOutput, calls=%fused_computation.10 | convolution fusion | flops 67371008 | bytes 9175296 | tf_op jit(solution)/shard_map/efij,efrj->eri/dot_general | solution.py:81
  214.8 4.9 %fusion.7 = f32[8,5,5]{1,2,0:T(8,128)S(1)} fusion(f32[5,64,8,128]{3,2,1,0:T(8,128)S(1)} %get-tuple-element.61), kind=kOutput, calls=%fused_computation.23 | convolution fusion | flops 19660800 | bytes 1311520 | tf_op jit(solution)/shard_map/icrn,jcrn->rij/dot_general | solution.py:86
  219.8 45.8 %psum.14 = f32[8,5,5]{1,2,0:T(8,128)S(1)} all-reduce(f32[8,5,5]{1,2,0:T(8,128)S(1)} %fusion.7), channel_id=1, replica_groups=mesh['gx'=16,'gy'=16] {'gx'}, use_global_device_ids=true, to_apply=%region_0.1 | all-reduce | flops 200 | bytes 1600 | tf_op jit(solution)/shard_map/psum | solution.py:92
  265.5 69.8 %psum.15 = f32[8,5,5]{1,2,0:T(8,128)S(1)} all-reduce(f32[8,5,5]{1,2,0:T(8,128)S(1)} %psum.14), channel_id=1, replica_groups=mesh['gx'=16,'gy'=16] {'gy'}, use_global_device_ids=true, to_apply=%region_1.2 | all-reduce | flops 200 | bytes 1600 | tf_op jit(solution)/shard_map/psum | solution.py:92
  335.6 3.0 custom-call.4
  (165 shorter events, 76.3 us)
Async XLA Ops:
  6.6 22.1 %collective-permute-start = (bf16[16,8,128]{2,1,0:T(8,128)(2,1)}, bf16[16,8,128]{2,1,0:T(8,128)(2,1)}, u32[]{:S(2)}, u32[]{:S(2)}) collective-permute-start(bf16[16,8,128]{2,1,0:T(8,128)(2,1)} %get-tuple-element.54), channel_id=1, source_target_pairs={{17,0},{18,1},{19,2},{20,3},{21,4},{22,5},{23,6},{24,7},{25,8},{26... | collective-permute-start | bytes 98312 | tf_op jit(solution)/shard_map/ppermute | solution.py:14
  13.3 23.9 %collective-permute-start.1 = (bf16[16,8,128]{2,1,0:T(8,128)(2,1)}, bf16[16,8,128]{2,1,0:T(8,128)(2,1)}, u32[]{:S(2)}, u32[]{:S(2)}) collective-permute-start(bf16[16,8,128]{2,1,0:T(8,128)(2,1)} %get-tuple-element.53), channel_id=1, source_target_pairs={{16,0},{17,1},{18,2},{19,3},{20,4},{21,5},{22,6},{23,7},{24,8},{25... | collective-permute-start | bytes 98312 | tf_op jit(solution)/shard_map/ppermute | solution.py:14
  15.2 25.5 %collective-permute-start.2 = (bf16[16,8,128]{2,1,0:T(8,128)(2,1)}, bf16[16,8,128]{2,1,0:T(8,128)(2,1)}, u32[]{:S(2)}, u32[]{:S(2)}) collective-permute-start(bf16[16,8,128]{2,1,0:T(8,128)(2,1)} %get-tuple-element.52), channel_id=1, source_target_pairs={{15,0},{16,1},{17,2},{18,3},{19,4},{20,5},{21,6},{22,7},{23,8},{24... | collective-permute-start | bytes 98312 | tf_op jit(solution)/shard_map/ppermute | solution.py:14
  17.1 25.5 %collective-permute-start.3 = (bf16[16,8,128]{2,1,0:T(8,128)(2,1)}, bf16[16,8,128]{2,1,0:T(8,128)(2,1)}, u32[]{:S(2)}, u32[]{:S(2)}) collective-permute-start(bf16[16,8,128]{2,1,0:T(8,128)(2,1)} %get-tuple-element.51), channel_id=1, source_target_pairs={{1,0},{2,1},{3,2},{4,3},{5,4},{6,5},{7,6},{8,7},{9,8},{10,9},{11,1... | collective-permute-start | bytes 98312 | tf_op jit(solution)/shard_map/ppermute | solution.py:14
  23.8 19.7 %collective-permute-start.4 = (bf16[16,8,128]{2,1,0:T(8,128)(2,1)}, bf16[16,8,128]{2,1,0:T(8,128)(2,1)}, u32[]{:S(2)}, u32[]{:S(2)}) collective-permute-start(bf16[16,8,128]{2,1,0:T(8,128)(2,1)} %get-tuple-element.50), channel_id=1, source_target_pairs={{0,1},{1,2},{2,3},{3,4},{4,5},{5,6},{6,7},{7,8},{8,9},{9,10},{10,1... | collective-permute-start | bytes 98312 | tf_op jit(solution)/shard_map/ppermute | solution.py:14
  28.7 14.7 %collective-permute-start.5 = (bf16[16,8,128]{2,1,0:T(8,128)(2,1)}, bf16[16,8,128]{2,1,0:T(8,128)(2,1)S(1)}, u32[]{:S(2)}, u32[]{:S(2)}) collective-permute-start(bf16[16,8,128]{2,1,0:T(8,128)(2,1)} %get-tuple-element.49), channel_id=1, source_target_pairs={{0,15},{1,16},{2,17},{3,18},{4,19},{5,20},{6,21},{7,22},{8,23},{9,... | collective-permute-start | bytes 98312 | tf_op jit(solution)/shard_map/ppermute | solution.py:14
  37.1 6.7 %collective-permute-start.6 = (bf16[16,8,128]{2,1,0:T(8,128)(2,1)}, bf16[16,8,128]{2,1,0:T(8,128)(2,1)S(1)}, u32[]{:S(2)}, u32[]{:S(2)}) collective-permute-start(bf16[16,8,128]{2,1,0:T(8,128)(2,1)} %get-tuple-element.48), channel_id=1, source_target_pairs={{0,16},{1,17},{2,18},{3,19},{4,20},{5,21},{6,22},{7,23},{8,24},{9,... | collective-permute-start | bytes 98312 | tf_op jit(solution)/shard_map/ppermute | solution.py:14
  40.7 11.6 %collective-permute-start.7 = (bf16[16,8,128]{2,1,0:T(8,128)(2,1)}, bf16[16,8,128]{2,1,0:T(8,128)(2,1)S(1)}, u32[]{:S(2)}, u32[]{:S(2)}) collective-permute-start(bf16[16,8,128]{2,1,0:T(8,128)(2,1)} %get-tuple-element.47), channel_id=1, source_target_pairs={{0,17},{1,18},{2,19},{3,20},{4,21},{5,22},{6,23},{7,24},{8,25},{9,... | collective-permute-start | bytes 98312 | tf_op jit(solution)/shard_map/ppermute | solution.py:14
  66.1 14.3 %collective-permute-start.8 = (bf16[16,8,128]{2,1,0:T(8,128)(2,1)S(1)}, bf16[16,8,128]{2,1,0:T(8,128)(2,1)S(1)}, u32[]{:S(2)}, u32[]{:S(2)}) collective-permute-start(bf16[16,8,128]{2,1,0:T(8,128)(2,1)S(1)} %get-tuple-element.46), channel_id=1, source_target_pairs={{17,0},{18,1},{19,2},{20,3},{21,4},{22,5},{23,6},{24,7},{25,8},{26... | collective-permute-start | bytes 98312 | tf_op jit(solution)/shard_map/ppermute | solution.py:14
  68.0 20.0 %collective-permute-start.9 = (bf16[16,8,128]{2,1,0:T(8,128)(2,1)S(1)}, bf16[16,8,128]{2,1,0:T(8,128)(2,1)S(1)}, u32[]{:S(2)}, u32[]{:S(2)}) collective-permute-start(bf16[16,8,128]{2,1,0:T(8,128)(2,1)S(1)} %get-tuple-element.45), channel_id=1, source_target_pairs={{16,0},{17,1},{18,2},{19,3},{20,4},{21,5},{22,6},{23,7},{24,8},{25... | collective-permute-start | bytes 98312 | tf_op jit(solution)/shard_map/ppermute | solution.py:14
  69.9 20.9 %collective-permute-start.10 = (bf16[16,8,128]{2,1,0:T(8,128)(2,1)S(1)}, bf16[16,8,128]{2,1,0:T(8,128)(2,1)S(1)}, u32[]{:S(2)}, u32[]{:S(2)}) collective-permute-start(bf16[16,8,128]{2,1,0:T(8,128)(2,1)S(1)} %get-tuple-element.44), channel_id=1, source_target_pairs={{15,0},{16,1},{17,2},{18,3},{19,4},{20,5},{21,6},{22,7},{23,8},{24... | collective-permute-start | bytes 98312 | tf_op jit(solution)/shard_map/ppermute | solution.py:14
  73.1 19.7 %collective-permute-start.11 = (bf16[16,8,128]{2,1,0:T(8,128)(2,1)S(1)}, bf16[16,8,128]{2,1,0:T(8,128)(2,1)S(1)}, u32[]{:S(2)}, u32[]{:S(2)}) collective-permute-start(bf16[16,8,128]{2,1,0:T(8,128)(2,1)S(1)} %get-tuple-element.43), channel_id=1, source_target_pairs={{1,0},{2,1},{3,2},{4,3},{5,4},{6,5},{7,6},{8,7},{9,8},{10,9},{11,1... | collective-permute-start | bytes 98312 | tf_op jit(solution)/shard_map/ppermute | solution.py:14
  78.5 14.4 %collective-permute-start.12 = (bf16[16,8,128]{2,1,0:T(8,128)(2,1)S(1)}, bf16[16,8,128]{2,1,0:T(8,128)(2,1)S(1)}, u32[]{:S(2)}, u32[]{:S(2)}) collective-permute-start(bf16[16,8,128]{2,1,0:T(8,128)(2,1)S(1)} %get-tuple-element.42), channel_id=1, source_target_pairs={{0,1},{1,2},{2,3},{3,4},{4,5},{5,6},{6,7},{7,8},{8,9},{9,10},{10,1... | collective-permute-start | bytes 98312 | tf_op jit(solution)/shard_map/ppermute | solution.py:14
  80.4 12.5 %collective-permute-start.13 = (bf16[16,8,128]{2,1,0:T(8,128)(2,1)S(1)}, bf16[16,8,128]{2,1,0:T(8,128)(2,1)S(1)}, u32[]{:S(2)}, u32[]{:S(2)}) collective-permute-start(bf16[16,8,128]{2,1,0:T(8,128)(2,1)S(1)} %get-tuple-element.41), channel_id=1, source_target_pairs={{0,15},{1,16},{2,17},{3,18},{4,19},{5,20},{6,21},{7,22},{8,23},{9,... | collective-permute-start | bytes 98312 | tf_op jit(solution)/shard_map/ppermute | solution.py:14
  88.0 6.4 %collective-permute-start.14 = (bf16[16,8,128]{2,1,0:T(8,128)(2,1)S(1)}, bf16[16,8,128]{2,1,0:T(8,128)(2,1)S(1)}, u32[]{:S(2)}, u32[]{:S(2)}) collective-permute-start(bf16[16,8,128]{2,1,0:T(8,128)(2,1)S(1)} %get-tuple-element.40), channel_id=1, source_target_pairs={{0,16},{1,17},{2,18},{3,19},{4,20},{5,21},{6,22},{7,23},{8,24},{9,... | collective-permute-start | bytes 98312 | tf_op jit(solution)/shard_map/ppermute | solution.py:14
  90.8 11.5 %collective-permute-start.15 = (bf16[16,8,128]{2,1,0:T(8,128)(2,1)S(1)}, bf16[16,8,128]{2,1,0:T(8,128)(2,1)S(1)}, u32[]{:S(2)}, u32[]{:S(2)}) collective-permute-start(bf16[16,8,128]{2,1,0:T(8,128)(2,1)S(1)} %get-tuple-element.39), channel_id=1, source_target_pairs={{0,17},{1,18},{2,19},{3,20},{4,21},{5,22},{6,23},{7,24},{8,25},{9,... | collective-permute-start | bytes 98312 | tf_op jit(solution)/shard_map/ppermute | solution.py:14
  116.1 14.7 %collective-permute-start.16 = (bf16[16,8,128]{2,1,0:T(8,128)(2,1)S(1)}, bf16[16,8,128]{2,1,0:T(8,128)(2,1)S(1)}, u32[]{:S(2)}, u32[]{:S(2)}) collective-permute-start(bf16[16,8,128]{2,1,0:T(8,128)(2,1)S(1)} %get-tuple-element.38), channel_id=1, source_target_pairs={{17,0},{18,1},{19,2},{20,3},{21,4},{22,5},{23,6},{24,7},{25,8},{26... | collective-permute-start | bytes 98312 | tf_op jit(solution)/shard_map/ppermute | solution.py:14
  118.6 20.0 %collective-permute-start.17 = (bf16[16,8,128]{2,1,0:T(8,128)(2,1)S(1)}, bf16[16,8,128]{2,1,0:T(8,128)(2,1)S(1)}, u32[]{:S(2)}, u32[]{:S(2)}) collective-permute-start(bf16[16,8,128]{2,1,0:T(8,128)(2,1)S(1)} %get-tuple-element.37), channel_id=1, source_target_pairs={{16,0},{17,1},{18,2},{19,3},{20,4},{21,5},{22,6},{23,7},{24,8},{25... | collective-permute-start | bytes 98312 | tf_op jit(solution)/shard_map/ppermute | solution.py:14
  120.6 20.9 %collective-permute-start.18 = (bf16[16,8,128]{2,1,0:T(8,128)(2,1)S(1)}, bf16[16,8,128]{2,1,0:T(8,128)(2,1)S(1)}, u32[]{:S(2)}, u32[]{:S(2)}) collective-permute-start(bf16[16,8,128]{2,1,0:T(8,128)(2,1)S(1)} %get-tuple-element.36), channel_id=1, source_target_pairs={{15,0},{16,1},{17,2},{18,3},{19,4},{20,5},{21,6},{22,7},{23,8},{24... | collective-permute-start | bytes 98312 | tf_op jit(solution)/shard_map/ppermute | solution.py:14
  123.6 19.8 %collective-permute-start.19 = (bf16[16,8,128]{2,1,0:T(8,128)(2,1)S(1)}, bf16[16,8,128]{2,1,0:T(8,128)(2,1)S(1)}, u32[]{:S(2)}, u32[]{:S(2)}) collective-permute-start(bf16[16,8,128]{2,1,0:T(8,128)(2,1)S(1)} %get-tuple-element.35), channel_id=1, source_target_pairs={{1,0},{2,1},{3,2},{4,3},{5,4},{6,5},{7,6},{8,7},{9,8},{10,9},{11,1... | collective-permute-start | bytes 98312 | tf_op jit(solution)/shard_map/ppermute | solution.py:14
  128.9 14.5 %collective-permute-start.20 = (bf16[16,8,128]{2,1,0:T(8,128)(2,1)S(1)}, bf16[16,8,128]{2,1,0:T(8,128)(2,1)S(1)}, u32[]{:S(2)}, u32[]{:S(2)}) collective-permute-start(bf16[16,8,128]{2,1,0:T(8,128)(2,1)S(1)} %get-tuple-element.34), channel_id=1, source_target_pairs={{0,1},{1,2},{2,3},{3,4},{4,5},{5,6},{6,7},{7,8},{8,9},{9,10},{10,1... | collective-permute-start | bytes 98312 | tf_op jit(solution)/shard_map/ppermute | solution.py:14
  130.9 12.6 %collective-permute-start.21 = (bf16[16,8,128]{2,1,0:T(8,128)(2,1)S(1)}, bf16[16,8,128]{2,1,0:T(8,128)(2,1)S(1)}, u32[]{:S(2)}, u32[]{:S(2)}) collective-permute-start(bf16[16,8,128]{2,1,0:T(8,128)(2,1)S(1)} %get-tuple-element.33), channel_id=1, source_target_pairs={{0,15},{1,16},{2,17},{3,18},{4,19},{5,20},{6,21},{7,22},{8,23},{9,... | collective-permute-start | bytes 98312 | tf_op jit(solution)/shard_map/ppermute | solution.py:14
  138.7 6.4 %collective-permute-start.22 = (bf16[16,8,128]{2,1,0:T(8,128)(2,1)S(1)}, bf16[16,8,128]{2,1,0:T(8,128)(2,1)S(1)}, u32[]{:S(2)}, u32[]{:S(2)}) collective-permute-start(bf16[16,8,128]{2,1,0:T(8,128)(2,1)S(1)} %get-tuple-element.32), channel_id=1, source_target_pairs={{0,16},{1,17},{2,18},{3,19},{4,20},{5,21},{6,22},{7,23},{8,24},{9,... | collective-permute-start | bytes 98312 | tf_op jit(solution)/shard_map/ppermute | solution.py:14
  141.5 11.5 %collective-permute-start.23 = (bf16[16,8,128]{2,1,0:T(8,128)(2,1)S(1)}, bf16[16,8,128]{2,1,0:T(8,128)(2,1)S(1)}, u32[]{:S(2)}, u32[]{:S(2)}) collective-permute-start(bf16[16,8,128]{2,1,0:T(8,128)(2,1)S(1)} %get-tuple-element.31), channel_id=1, source_target_pairs={{0,17},{1,18},{2,19},{3,20},{4,21},{5,22},{6,23},{7,24},{8,25},{9,... | collective-permute-start | bytes 98312 | tf_op jit(solution)/shard_map/ppermute | solution.py:14
  166.8 14.4 %collective-permute-start.24 = (bf16[16,8,128]{2,1,0:T(8,128)(2,1)S(1)}, bf16[16,8,128]{2,1,0:T(8,128)(2,1)S(1)}, u32[]{:S(2)}, u32[]{:S(2)}) collective-permute-start(bf16[16,8,128]{2,1,0:T(8,128)(2,1)S(1)} %get-tuple-element.30), channel_id=1, source_target_pairs={{17,0},{18,1},{19,2},{20,3},{21,4},{22,5},{23,6},{24,7},{25,8},{26... | collective-permute-start | bytes 98312 | tf_op jit(solution)/shard_map/ppermute | solution.py:14
  169.3 20.0 %collective-permute-start.25 = (bf16[16,8,128]{2,1,0:T(8,128)(2,1)S(1)}, bf16[16,8,128]{2,1,0:T(8,128)(2,1)S(1)}, u32[]{:S(2)}, u32[]{:S(2)}) collective-permute-start(bf16[16,8,128]{2,1,0:T(8,128)(2,1)S(1)} %get-tuple-element.29), channel_id=1, source_target_pairs={{16,0},{17,1},{18,2},{19,3},{20,4},{21,5},{22,6},{23,7},{24,8},{25... | collective-permute-start | bytes 98312 | tf_op jit(solution)/shard_map/ppermute | solution.py:14
  171.2 20.9 %collective-permute-start.26 = (bf16[16,8,128]{2,1,0:T(8,128)(2,1)S(1)}, bf16[16,8,128]{2,1,0:T(8,128)(2,1)S(1)}, u32[]{:S(2)}, u32[]{:S(2)}) collective-permute-start(bf16[16,8,128]{2,1,0:T(8,128)(2,1)S(1)} %get-tuple-element.28), channel_id=1, source_target_pairs={{15,0},{16,1},{17,2},{18,3},{19,4},{20,5},{21,6},{22,7},{23,8},{24... | collective-permute-start | bytes 98312 | tf_op jit(solution)/shard_map/ppermute | solution.py:14
  173.9 20.3 %collective-permute-start.27 = (bf16[16,8,128]{2,1,0:T(8,128)(2,1)S(1)}, bf16[16,8,128]{2,1,0:T(8,128)(2,1)S(1)}, u32[]{:S(2)}, u32[]{:S(2)}) collective-permute-start(bf16[16,8,128]{2,1,0:T(8,128)(2,1)S(1)} %get-tuple-element.27), channel_id=1, source_target_pairs={{1,0},{2,1},{3,2},{4,3},{5,4},{6,5},{7,6},{8,7},{9,8},{10,9},{11,1... | collective-permute-start | bytes 98312 | tf_op jit(solution)/shard_map/ppermute | solution.py:14
  179.3 15.0 %collective-permute-start.28 = (bf16[16,8,128]{2,1,0:T(8,128)(2,1)S(1)}, bf16[16,8,128]{2,1,0:T(8,128)(2,1)S(1)}, u32[]{:S(2)}, u32[]{:S(2)}) collective-permute-start(bf16[16,8,128]{2,1,0:T(8,128)(2,1)S(1)} %get-tuple-element.26), channel_id=1, source_target_pairs={{0,1},{1,2},{2,3},{3,4},{4,5},{5,6},{6,7},{7,8},{8,9},{9,10},{10,1... | collective-permute-start | bytes 98312 | tf_op jit(solution)/shard_map/ppermute | solution.py:14
  181.2 13.1 %collective-permute-start.29 = (bf16[16,8,128]{2,1,0:T(8,128)(2,1)S(1)}, bf16[16,8,128]{2,1,0:T(8,128)(2,1)S(1)}, u32[]{:S(2)}, u32[]{:S(2)}) collective-permute-start(bf16[16,8,128]{2,1,0:T(8,128)(2,1)S(1)} %get-tuple-element.25), channel_id=1, source_target_pairs={{0,15},{1,16},{2,17},{3,18},{4,19},{5,20},{6,21},{7,22},{8,23},{9,... | collective-permute-start | bytes 98312 | tf_op jit(solution)/shard_map/ppermute | solution.py:14
  189.3 6.4 %collective-permute-start.30 = (bf16[16,8,128]{2,1,0:T(8,128)(2,1)S(1)}, bf16[16,8,128]{2,1,0:T(8,128)(2,1)S(1)}, u32[]{:S(2)}, u32[]{:S(2)}) collective-permute-start(bf16[16,8,128]{2,1,0:T(8,128)(2,1)S(1)} %get-tuple-element.24), channel_id=1, source_target_pairs={{0,16},{1,17},{2,18},{3,19},{4,20},{5,21},{6,22},{7,23},{8,24},{9,... | collective-permute-start | bytes 98312 | tf_op jit(solution)/shard_map/ppermute | solution.py:14
  192.1 11.5 %collective-permute-start.31 = (bf16[16,8,128]{2,1,0:T(8,128)(2,1)S(1)}, bf16[16,8,128]{2,1,0:T(8,128)(2,1)S(1)}, u32[]{:S(2)}, u32[]{:S(2)}) collective-permute-start(bf16[16,8,128]{2,1,0:T(8,128)(2,1)S(1)} %get-tuple-element.23), channel_id=1, source_target_pairs={{0,17},{1,18},{2,19},{3,20},{4,21},{5,22},{6,23},{7,24},{8,25},{9,... | collective-permute-start | bytes 98312 | tf_op jit(solution)/shard_map/ppermute | solution.py:14
  (14 other events, 412.0 us)
